TPU v7x, 32 devices: a whole 2x2x4 slice. The times are simulated.
32 devices in a mesh: grp: 4 (over x, core), dev: 8 (over z, y).
Axes of the slice: x: 2, y: 2, z: 4, core: 2. Of those that a mesh axis runs over, the one named last changes fastest.
Arguments:
- coefficients: float32 [2, 8, 64, 4096], P(None, None, None, ('grp', 'dev')), may hold values from -6 to 6
- spatial_root: int32 [64], replicated, may hold values from 0 to 1023
- frequency_root: int32 [64], replicated, may hold values from 0 to 255
Outputs:
- result: float32 [2, 8, 64, 4096], P(None, None, None, ('grp', 'dev'))
All inputs are finite; a program needn't handle non-finite values.
Results may differ from a plain program's by a relative error of at most 0.002.
Values sent between devices are 32-bit elements; how exact they have to be, the bound alone decides.
A program may use at most 64 MiB of HBM per device.

v0:
```python
import math
import jax
import jax.numpy as jnp
from jax import lax
from jax.sharding import PartitionSpec as P

LEVELS = 12
HIGHEST = lax.Precision.HIGHEST


def partner_2(block, axis, distance):
    count = lax.axis_size(axis)
    route = []
    for low in range(count):
        high = low | 1 << distance
        if high != low and high < count:
            route += [(low, high), (high, low)]
    return lax.ppermute(block, axis, route)


def cheb_nodes():
    node_order = jnp.arange(8, dtype=jnp.float32)
    return 0.5 - 0.5 * jnp.cos(math.pi * (2.0 * node_order + 1.0) / 16.0)


def lagrange_table(half_cell):
    points = cheb_nodes()
    target = (points + half_cell) / 2.0
    diagonal = jnp.arange(8)[:, None] == jnp.arange(8)[None, :]
    numerator = jnp.where(
        diagonal[None, :, :], jnp.float32(1.0), target[:, None, None] - points[None, None, :]
    )
    denominator = jnp.where(diagonal, jnp.float32(1.0), points[:, None] - points[None, :])
    return jnp.prod(numerator, axis=2) / jnp.prod(denominator, axis=1)[None, :]


def interp_tables():
    halves = [lagrange_table(0.0), lagrange_table(1.0)]
    return jnp.stack(
        [jnp.kron(halves[quadrant % 2], halves[quadrant // 2]) for quadrant in range(4)]
    )


def pair_digits(pair_index, pairs_dev, devices_dev):
    quarter = pairs_dev // 4
    within = pair_index % pairs_dev
    device = pair_index // pairs_dev % devices_dev
    group_id = pair_index // (pairs_dev * devices_dev)
    places = [device % 4, group_id % 4, within // quarter]
    return (places, device // 4 * quarter + within % quarter)


def pair_boxes(pair_index, level_step, box_roots, pairs_dev, devices_dev, levels):
    places, _ = pair_digits(pair_index, pairs_dev, devices_dev)
    coarse_space = levels // 2 - 1
    coarse_wave = levels // 2 - 2
    space_row = box_roots[0] // 2**coarse_space
    space_column = box_roots[0] % 2**coarse_space
    for position in range(level_step):
        space_row = 2 * space_row + places[position] % 2
        space_column = 2 * space_column + places[position] // 2
    wave_row = box_roots[1] // 2**coarse_wave
    wave_column = box_roots[1] % 2**coarse_wave
    for position in range(2, level_step - 1, -1):
        wave_row = 2 * wave_row + places[position] % 2
        wave_column = 2 * wave_column + places[position] // 2
    space_side = 0.5 ** (coarse_space + level_step)
    wave_side = float(2**levels) / float(2 ** (coarse_wave + 3 - level_step))
    offset = -0.5 * float(2**levels)
    space_box = (
        space_row.astype(jnp.float32) * space_side,
        space_column.astype(jnp.float32) * space_side,
        space_side,
    )
    wave_box = (
        offset + wave_row.astype(jnp.float32) * wave_side,
        offset + wave_column.astype(jnp.float32) * wave_side,
        wave_side,
    )
    return (space_box, wave_box)


def box_points(square):
    points = cheb_nodes()
    first_axis = jnp.repeat(points, 8)
    second_axis = jnp.tile(points, 8)
    return (
        square[0][None, :] + square[2] * first_axis[:, None],
        square[1][None, :] + square[2] * second_axis[:, None],
    )


def box_center(square):
    return (square[0] + 0.5 * square[2], square[1] + 0.5 * square[2])


def phase_angle(first_space, second_space, first_wave, second_wave):
    two_pi = 2.0 * math.pi
    wave_speed = 16.0 * math.pi
    speed_one = (
        2.0 + jnp.sin(wave_speed * first_space) * jnp.sin(wave_speed * second_space)
    ) / 16.0
    speed_two = (
        2.0 + jnp.cos(wave_speed * first_space) * jnp.cos(wave_speed * second_space)
    ) / 16.0
    radial = jnp.sqrt(
        speed_one * speed_one * first_wave * first_wave
        + speed_two * speed_two * second_wave * second_wave
    )
    return two_pi * (first_space * first_wave + second_space * second_wave + radial)


def rotate(values, turn_angle):
    cosine = jnp.cos(turn_angle)
    sine_part = jnp.sin(turn_angle)
    return jnp.stack(
        [values[0] * cosine - values[1] * sine_part, values[0] * sine_part + values[1] * cosine]
    )


def pre_merge(
    children, new_index, new_roots, child_index, child_roots, pairs_dev, devices_dev, levels
):
    space_box, wave_box = pair_boxes(new_index, 1, new_roots, pairs_dev, devices_dev, levels)
    center_one, center_two = box_center(space_box)
    turned = []
    for child_id in range(4):
        _, child_wave = pair_boxes(
            child_index[child_id],
            0,
            (child_roots[0][child_id], child_roots[1][child_id]),
            pairs_dev,
            devices_dev,
            levels,
        )
        wave_one, wave_two = box_points(child_wave)
        turned.append(
            rotate(
                children[child_id],
                -phase_angle(center_one[None, :], center_two[None, :], wave_one, wave_two),
            )
        )
    summed = jnp.einsum("cst,caksm->aktm", interp_tables(), jnp.stack(turned), precision=HIGHEST)
    wave_one, wave_two = box_points(wave_box)
    return rotate(summed, phase_angle(center_one[None, :], center_two[None, :], wave_one, wave_two))


def switch_step(values, pair_index, box_roots, pairs_dev, devices_dev, levels):
    space_box, wave_box = pair_boxes(pair_index, 1, box_roots, pairs_dev, devices_dev, levels)
    space_one, space_two = box_points(space_box)
    wave_one, wave_two = box_points(wave_box)
    kernel_angle = phase_angle(
        space_one[:, None, :], space_two[:, None, :], wave_one[None, :, :], wave_two[None, :, :]
    )
    cosine = jnp.cos(kernel_angle)
    sine_part = jnp.sin(kernel_angle)
    real_part = jnp.einsum("tsm,ksm->ktm", cosine, values[0], precision=HIGHEST) - jnp.einsum(
        "tsm,ksm->ktm", sine_part, values[1], precision=HIGHEST
    )
    imag_part = jnp.einsum("tsm,ksm->ktm", sine_part, values[0], precision=HIGHEST) + jnp.einsum(
        "tsm,ksm->ktm", cosine, values[1], precision=HIGHEST
    )
    return jnp.stack([real_part, imag_part]) / 64.0


def post_terms(values, pair_index, box_roots, level_step, pairs_dev, devices_dev, levels):
    space_box, wave_box = pair_boxes(
        pair_index, level_step, box_roots, pairs_dev, devices_dev, levels
    )
    space_one, space_two = box_points(space_box)
    center_one, center_two = box_center(wave_box)
    return rotate(
        values, -phase_angle(space_one, space_two, center_one[None, :], center_two[None, :])
    )


def post_finish(merged, pair_index, box_roots, level_step, pairs_dev, devices_dev, levels):
    space_box, wave_box = pair_boxes(
        pair_index, level_step, box_roots, pairs_dev, devices_dev, levels
    )
    space_one, space_two = box_points(space_box)
    center_one, center_two = box_center(wave_box)
    return rotate(
        merged, phase_angle(space_one, space_two, center_one[None, :], center_two[None, :])
    )


def lookup_roots(pair_index, spatial_root, frequency_root, pairs_dev, devices_dev):
    _, block_id = pair_digits(pair_index, pairs_dev, devices_dev)
    matches = block_id[..., None] == jnp.arange(spatial_root.shape[0], dtype=jnp.int32)
    return (
        jnp.sum(jnp.where(matches, spatial_root, 0), axis=-1),
        jnp.sum(jnp.where(matches, frequency_root, 0), axis=-1),
    )


def middle_levels(first_level, held_index, held_roots, group_id, pairs_dev, devices_dev, total_fn):
    switched = switch_step(first_level, held_index, held_roots, pairs_dev, devices_dev, LEVELS)
    child_terms = post_terms(switched, held_index, held_roots, 1, pairs_dev, devices_dev, LEVELS)
    summed = total_fn(child_terms)
    local_interp = lax.dynamic_index_in_dim(interp_tables(), group_id, 0, keepdims=False)
    spread_level = jnp.einsum("ts,aksm->aktm", local_interp, summed, precision=HIGHEST)
    return post_finish(spread_level, held_index, held_roots, 2, pairs_dev, devices_dev, LEVELS)


def per_device(coefficients, spatial_root, frequency_root):
    rhs_count = coefficients.shape[1]
    rank_count = coefficients.shape[2]
    pairs_dev = coefficients.shape[3]
    devices_dev = lax.axis_size("dev")
    group_id = lax.axis_index("grp")
    device_id = lax.axis_index("dev")
    base_index = group_id * (devices_dev * pairs_dev)
    own_index = base_index + device_id * pairs_dev + jnp.arange(pairs_dev, dtype=jnp.int32)
    own_roots = lookup_roots(own_index, spatial_root, frequency_root, pairs_dev, devices_dev)
    stacked = coefficients[None]
    for bit_number in range(2):
        partner = partner_2(stacked, "dev", bit_number)
        upper_half = device_id // 2**bit_number % 2
        stacked = jnp.where(
            upper_half == 1,
            jnp.concatenate([partner, stacked]),
            jnp.concatenate([stacked, partner]),
        )
    child_index = (
        own_index[None, :] + (jnp.arange(4, dtype=jnp.int32)[:, None] - device_id % 4) * pairs_dev
    )
    child_roots = lookup_roots(child_index, spatial_root, frequency_root, pairs_dev, devices_dev)
    first_level = pre_merge(
        stacked, own_index, own_roots, child_index, child_roots, pairs_dev, devices_dev, LEVELS
    )
    second = middle_levels(
        first_level,
        own_index,
        own_roots,
        group_id,
        pairs_dev,
        devices_dev,
        lambda terms: lax.psum(terms, "grp"),
    )
    child_terms = post_terms(second, own_index, own_roots, 2, pairs_dev, devices_dev, LEVELS)
    summed = jnp.sum(child_terms.reshape(2, rhs_count, rank_count, 4, pairs_dev // 4), axis=3)
    spread_last = jnp.einsum("jts,aksm->aktjm", interp_tables(), summed, precision=HIGHEST).reshape(
        2, rhs_count, rank_count, pairs_dev
    )
    return post_finish(spread_last, own_index, own_roots, 3, pairs_dev, devices_dev, LEVELS)


def solution(mesh):
    return jax.shard_map(
        per_device,
        mesh=mesh,
        in_specs=(P(None, None, None, ("grp", "dev")), P(), P()),
        out_specs=P(None, None, None, ("grp", "dev")),
        check_vma=False,
    )
```

profile of v0, /device:TPU:0, one launch (start us, length us, event | category | flops | bytes accessed | tf_op | source)
XLA Modules:
  0.0 217.6 jit_solution(8685077930100766251)
XLA Ops:
  6.5 3.0 %collective-permute-start = (f32[1,2,8,64,128]{4,3,2,1,0:T(8,128)}, f32[1,2,8,64,128]{4,3,2,1,0:T(8,128)S(1)}, u32[]{:S(2)}, u32[]{:S(2)}) collective-permute-start(f32[1,2,8,64,128]{4,3,2,1,0:T(8,128)} %bitcast.157), channel_id=1, source_target_pairs={{0,1},{1,0},{2,3},{3,2},{4,5},{5,4},{6,7},{7,6},{8,9},{9,8},{10,11... | collective-permute-start | bytes 1572872 | tf_op jit(solution)/shard_map/ppermute | solution.py:18
  9.8 0.8 select_reduce_fusion.4
  10.8 0.8 select_reduce_fusion
  11.6 0.2 select_reduce_fusion.5
  11.8 0.3 select_reduce_fusion.2
  12.8 0.5 fusion.152
  13.3 0.1 broadcast_multiply_fusion.1
  13.4 8.3 %collective-permute-done = f32[1,2,8,64,128]{4,3,2,1,0:T(8,128)S(1)} collective-permute-done((f32[1,2,8,64,128]{4,3,2,1,0:T(8,128)}, f32[1,2,8,64,128]{4,3,2,1,0:T(8,128)S(1)}, u32[]{:S(2)}, u32[]{:S(2)}) %collective-permute-start) | collective-permute-done | bytes 524320 | tf_op jit(solution)/shard_map/ppermute | solution.py:18
  21.7 1.4 maximum_select_fusion.1
  23.1 1.9 collective-permute-start.1
  26.2 0.8 fusion.150
  28.0 0.5 fusion.140
  28.4 19.0 %collective-permute-done.1 = f32[2,2,8,64,128]{4,3,2,1,0:T(8,128)S(1)} collective-permute-done((f32[2,2,8,64,128]{4,3,2,1,0:T(8,128)S(1)}, f32[2,2,8,64,128]{4,3,2,1,0:T(8,128)S(1)}, u32[]{:S(2)}, u32[]{:S(2)}) %collective-permute-start.1) | collective-permute-done | bytes 1048608 | tf_op jit(solution)/shard_map/ppermute | solution.py:18
  47.5 0.3 maximum_select_fusion
  47.8 0.2 multiply_subtract_fusion.8
  48.3 1.5 fusion.46
  49.8 0.2 copy.63
  50.1 0.2 copy.62
  50.3 29.0 %fusion.2 = f32[128,8,64]{2,1,0:T(8,128)S(1)} fusion(f32[8,64,128]{1,0,2:T(8,128)S(1)} %copy.63, f32[64,128]{0,1:T(8,128)S(1)} %copy.61, f32[64,128]{0,1:T(8,128)S(1)} %copy.60, f32[64,128]{0,1:T(8,128)S(1)} %copy.59, f32[64,128]{0,1:T(8,128)S(1)} %copy.58, f32[64,128]{0,1:T(8,128)S(1)} %copy.57, f32[64,128]{0,1:T(8,128)S(1)} %copy.56), kind=kOutput, calls=%fused_computation.3 | convolution fusion | flops 55574528 | bytes 720896 | tf_op jit(solution)/shard_map/tsm,ksm->ktm/dot_general | solution.py:160
  79.3 28.8 %fusion.4 = f32[128,8,64]{2,1,0:T(8,128)S(1)} fusion(f32[8,64,128]{1,0,2:T(8,128)S(1)} %copy.62, f32[64,128]{0,1:T(8,128)S(1)} %copy.61, f32[64,128]{0,1:T(8,128)S(1)} %copy.60, f32[64,128]{0,1:T(8,128)S(1)} %copy.59, f32[64,128]{0,1:T(8,128)S(1)} %copy.58, f32[64,128]{0,1:T(8,128)S(1)} %copy.57, f32[64,128]{0,1:T(8,128)S(1)} %copy.56), kind=kOutput, calls=%fused_computation.4 | convolution fusion | flops 55574528 | bytes 720896 | tf_op jit(solution)/shard_map/tsm,ksm->ktm/dot_general | solution.py:157
  108.1 29.0 %fusion.58 = f32[1,8,64,128]{2,1,3,0:T(8,128)S(1)} fusion(f32[128,8,64]{2,1,0:T(8,128)S(1)} %fusion.2, f32[8,64,128]{1,0,2:T(8,128)S(1)} %copy.62, f32[64,128]{0,1:T(8,128)S(1)} %copy.61, f32[64,128]{0,1:T(8,128)S(1)} %copy.60, f32[64,128]{0,1:T(8,128)S(1)} %copy.59, f32[64,128]{0,1:T(8,128)S(1)} %copy.58, f32[64,128]{0,1:T(8,128)S(1)} %copy.57, ...), kind=kOutput, calls=%fused_computation.50 | convolution fusion | flops 55640064 | bytes 983040 | tf_op jit(solution)/shard_map/tsm,ksm->ktm/dot_general | solution.py:160
  137.1 29.0 %fusion.52 = f32[1,8,64,128]{2,1,3,0:T(8,128)S(1)} fusion(f32[128,8,64]{2,1,0:T(8,128)S(1)} %fusion.4, f32[8,64,128]{1,0,2:T(8,128)S(1)} %copy.63, f32[64,128]{0,1:T(8,128)S(1)} %copy.61, f32[64,128]{0,1:T(8,128)S(1)} %copy.60, f32[64,128]{0,1:T(8,128)S(1)} %copy.59, f32[64,128]{0,1:T(8,128)S(1)} %copy.58, f32[64,128]{0,1:T(8,128)S(1)} %copy.57, ...), kind=kOutput, calls=%fused_computation.48 | convolution fusion | flops 55640064 | bytes 983040 | tf_op jit(solution)/shard_map/tsm,ksm->ktm/dot_general | solution.py:157
  166.3 1.1 pad_maximum_fusion
  167.7 0.6 fusion.138
  168.3 36.7 %all-reduce.2.cloned.1.call-done = f32[2,8,64,128]{2,1,3,0:T(8,128)} async-done(((f32[2,8,64,128]{2,1,3,0:T(8,128)}), f32[2,8,64,128]{2,1,3,0:T(8,128)}) %all-reduce.2.cloned.1.call-update) | async-done | bytes 524304 | tf_op jit(solution)/shard_map/psum | solution.py:239
  205.1 2.6 %convolution_bitcast_fusion.1 = f32[2,8,64,128]{3,2,1,0:T(8,128)S(1)} fusion(f32[2,8,64,128]{2,1,3,0:T(8,128)} %all-reduce.2.cloned.1.call-done, f32[4,64,64]{1,2,0:T(8,128)S(1)} %constant_dynamic-update-slice_fusion, s32[]{:T(128)S(6)} %select_n.1084), kind=kOutput, calls=%fused_computation.46 | convolution fusion | flops 100663296 | bytes 1081348 | tf_op jit(solution)/shard_map/ts,aksm->aktm/dot_general | solution.py:202
  207.8 0.2 copy.71
  208.0 0.2 copy.70
  208.3 1.0 convolution_bitcast_fusion
  209.4 0.2 copy.74
  209.6 0.2 copy.73
  209.9 0.8 pad_maximum_fusion.1
  (74 shorter events, 4.3 us)
Async XLA Ops:
  6.5 198.5 %all-reduce.2.cloned.1.call-start = ((), (), s32[]{:S(2)}) async-start(), calls=%async_computation | async-start | bytes 2097152 | tf_op jit(solution)/shard_map/psum | solution.py:239
  6.5 15.1 %collective-permute-start = (f32[1,2,8,64,128]{4,3,2,1,0:T(8,128)}, f32[1,2,8,64,128]{4,3,2,1,0:T(8,128)S(1)}, u32[]{:S(2)}, u32[]{:S(2)}) collective-permute-start(f32[1,2,8,64,128]{4,3,2,1,0:T(8,128)} %bitcast.157), channel_id=1, source_target_pairs={{0,1},{1,0},{2,3},{3,2},{4,5},{5,4},{6,7},{7,6},{8,9},{9,8},{10,11... | collective-permute-start | bytes 1572872 | tf_op jit(solution)/shard_map/ppermute | solution.py:18
  23.1 24.4 %collective-permute-start.1 = (f32[2,2,8,64,128]{4,3,2,1,0:T(8,128)S(1)}, f32[2,2,8,64,128]{4,3,2,1,0:T(8,128)S(1)}, u32[]{:S(2)}, u32[]{:S(2)}) collective-permute-start(f32[2,2,8,64,128]{4,3,2,1,0:T(8,128)S(1)} %maximum_select_fusion.1), channel_id=1, source_target_pairs={{0,2},{2,0},{1,3},{3,1},{4,6},{6,4},{5,7},{7,5},{8,10},{10,8},{9,1... | collective-permute-start | bytes 3145736 | tf_op jit(solution)/shard_map/ppermute | solution.py:18
Sparse Core Ops, SparseCore 0:
  167.6 37.4 all-reduce.1
where the time goes:
time: 218 us
  matrix products  121 us (56%)
  waiting for transfers between devices  64 us (29%)
  between operations  14 us (6%)
  other arithmetic  10 us (5%)
  starting transfers between devices  4.86 us (2%)
  local copies, waits for them, and re-layouts  3.9 us (2%)
    psum x1, waiting for transfers between devices, per_device(): lax.psum(terms, 'grp')  36.7 us
    dot_general x1, matrix products, switch_step(): jnp.einsum('tsm,ksm->ktm', cosine, values[1], precision=HIGHEST)  29 us
    dot_general x1, matrix products, switch_step(): jnp.einsum('tsm,ksm->ktm', sine_part, values[0], precision=HIGHEST)  29 us
    dot_general x1, matrix products, switch_step(): jnp.einsum('tsm,ksm->ktm', sine_part, values[1], precision=HIGHEST)  29 us
    dot_general x1, matrix products, switch_step(): jnp.einsum('tsm,ksm->ktm', cosine, values[0], precision=HIGHEST)  28.8 us
    ppermute x2, waiting for transfers between devices, partner_2(): return lax.ppermute(block, axis, route)  27.3 us
    ppermute x2, starting transfers between devices, partner_2(): return lax.ppermute(block, axis, route)  4.86 us
  transfers between devices with their start and end apart: 3, of which 3 were waited for; matrix products, arithmetic and copies ran while one was open for 4% of the time, Pallas kernels for 0%

commit v1 on v0

--- a/solution.py
+++ b/solution.py
@@ -6,6 +6,12 @@
 
 LEVELS = 12
 HIGHEST = lax.Precision.HIGHEST
+
+
+def add_all(array, name):
+    blocks = lax.all_gather(array, name, axis=0, tiled=False)
+    total = blocks.sum(axis=0)
+    return total
 
 
 def partner_2(block, axis, distance):
@@ -236,7 +242,7 @@
         group_id,
         pairs_dev,
         devices_dev,
-        lambda terms: lax.psum(terms, "grp"),
+        lambda terms: add_all(terms, "grp"),
     )
     child_terms = post_terms(second, own_index, own_roots, 2, pairs_dev, devices_dev, LEVELS)
     summed = jnp.sum(child_terms.reshape(2, rhs_count, rank_count, 4, pairs_dev // 4), axis=3)

time: 218 us -> 203 us (0.931)
  waiting for transfers between devices: 64 us -> 51.1 us
    psum x1 -> x0, waiting for transfers between devices: 36.7 us -> none  [per_device(): lax.psum(terms, 'grp')]
    all_gather x0 -> x1, waiting for transfers between devices: none -> 22.1 us  [add_all(): blocks = lax.all_gather(array, name, axis=0, tiled=False)]
where the time goes in v1:
time: 203 us; the launch traced here: 202 us
  matrix products  119 us (59%)
  waiting for transfers between devices  51.1 us (25%)
  between operations  14 us (7%)
  other arithmetic  8.82 us (4%)
  local copies, waits for them, and re-layouts  5.04 us (2%)
  starting transfers between devices  4.8 us (2%)
    dot_general x1, matrix products, switch_step(): jnp.einsum('tsm,ksm->ktm', cosine, values[1], precision=HIGHEST)  29 us
    dot_general x1, matrix products, switch_step(): jnp.einsum('tsm,ksm->ktm', sine_part, values[0], precision=HIGHEST)  29 us
    dot_general x1, matrix products, switch_step(): jnp.einsum('tsm,ksm->ktm', sine_part, values[1], precision=HIGHEST)  29 us
    ppermute x2, waiting for transfers between devices, partner_2(): return lax.ppermute(block, axis, route)  28.9 us
    dot_general x1, matrix products, switch_step(): jnp.einsum('tsm,ksm->ktm', cosine, values[0], precision=HIGHEST)  28.8 us
    all_gather x1, waiting for transfers between devices, add_all(): blocks = lax.all_gather(array, name, axis=0, tiled=False)  22.1 us
    ppermute x2, starting transfers between devices, partner_2(): return lax.ppermute(block, axis, route)  4.79 us
  transfers between devices with their start and end apart: 3, of which 3 were waited for; matrix products, arithmetic and copies ran while one was open for 4% of the time, Pallas kernels for 0%

profile of v1, /device:TPU:0, one launch (start us, length us, event | category | flops | bytes accessed | tf_op | source)
XLA Modules:
  0.0 202.5 jit_solution(16782362663185226382)
XLA Ops:
  6.5 3.0 %collective-permute-start = (f32[1,2,8,64,128]{4,3,2,1,0:T(8,128)}, f32[1,2,8,64,128]{4,3,2,1,0:T(8,128)S(1)}, u32[]{:S(2)}, u32[]{:S(2)}) collective-permute-start(f32[1,2,8,64,128]{4,3,2,1,0:T(8,128)} %bitcast.160), channel_id=1, source_target_pairs={{0,1},{1,0},{2,3},{3,2},{4,5},{5,4},{6,7},{7,6},{8,9},{9,8},{10,11... | collective-permute-start | bytes 1572872 | tf_op jit(solution)/shard_map/ppermute | solution.py:24
  9.9 0.8 select_reduce_fusion.4
  11.3 0.2 select_reduce_fusion.5
  11.5 0.3 select_reduce_fusion.2
  12.0 0.1 broadcast_multiply_fusion.1
  12.2 0.1 mul.2618
  12.9 0.5 fusion.151
  14.0 7.8 %collective-permute-done = f32[1,2,8,64,128]{4,3,2,1,0:T(8,128)S(1)} collective-permute-done((f32[1,2,8,64,128]{4,3,2,1,0:T(8,128)}, f32[1,2,8,64,128]{4,3,2,1,0:T(8,128)S(1)}, u32[]{:S(2)}, u32[]{:S(2)}) %collective-permute-start) | collective-permute-done | bytes 524320 | tf_op jit(solution)/shard_map/ppermute | solution.py:24
  21.9 1.8 collective-permute-start.1
  23.7 0.8 fusion.149
  25.1 21.1 %collective-permute-done.1 = f32[2,2,8,64,128]{4,3,2,1,0:T(8,128)S(1)} collective-permute-done((f32[2,2,8,64,128]{4,3,2,1,0:T(8,128)S(1)}, f32[2,2,8,64,128]{4,3,2,1,0:T(8,128)S(1)}, u32[]{:S(2)}, u32[]{:S(2)}) %collective-permute-start.1) | collective-permute-done | bytes 1048608 | tf_op jit(solution)/shard_map/ppermute | solution.py:24
  46.2 0.3 maximum_select_fusion
  46.5 0.2 multiply_subtract_fusion.8
  47.0 1.5 fusion.46
  48.6 0.2 copy.87
  48.9 0.2 copy.86
  49.1 29.0 %fusion.2 = f32[128,8,64]{2,1,0:T(8,128)S(1)} fusion(f32[8,64,128]{1,0,2:T(8,128)S(1)} %copy.87, f32[64,128]{0,1:T(8,128)S(1)} %copy.85, f32[64,128]{0,1:T(8,128)S(1)} %copy.84, f32[64,128]{0,1:T(8,128)S(1)} %copy.83, f32[64,128]{0,1:T(8,128)S(1)} %copy.82, f32[64,128]{0,1:T(8,128)S(1)} %copy.81, f32[64,128]{0,1:T(8,128)S(1)} %copy.80), kind=kOutput, calls=%fused_computation.3 | convolution fusion | flops 55574528 | bytes 720896 | tf_op jit(solution)/shard_map/tsm,ksm->ktm/dot_general | solution.py:166
  78.1 28.8 %fusion.4 = f32[128,8,64]{2,1,0:T(8,128)S(1)} fusion(f32[8,64,128]{1,0,2:T(8,128)S(1)} %copy.86, f32[64,128]{0,1:T(8,128)S(1)} %copy.85, f32[64,128]{0,1:T(8,128)S(1)} %copy.84, f32[64,128]{0,1:T(8,128)S(1)} %copy.83, f32[64,128]{0,1:T(8,128)S(1)} %copy.82, f32[64,128]{0,1:T(8,128)S(1)} %copy.81, f32[64,128]{0,1:T(8,128)S(1)} %copy.80), kind=kOutput, calls=%fused_computation.4 | convolution fusion | flops 55574528 | bytes 720896 | tf_op jit(solution)/shard_map/tsm,ksm->ktm/dot_general | solution.py:163
  106.9 29.0 %fusion.58 = f32[1,8,64,128]{2,1,3,0:T(8,128)S(1)} fusion(f32[128,8,64]{2,1,0:T(8,128)S(1)} %fusion.2, f32[8,64,128]{1,0,2:T(8,128)S(1)} %copy.86, f32[64,128]{0,1:T(8,128)S(1)} %copy.85, f32[64,128]{0,1:T(8,128)S(1)} %copy.84, f32[64,128]{0,1:T(8,128)S(1)} %copy.83, f32[64,128]{0,1:T(8,128)S(1)} %copy.82, f32[64,128]{0,1:T(8,128)S(1)} %copy.81, ...), kind=kOutput, calls=%fused_computation.50 | convolution fusion | flops 55640064 | bytes 983040 | tf_op jit(solution)/shard_map/tsm,ksm->ktm/dot_general | solution.py:166
  135.9 29.0 %fusion.52 = f32[1,8,64,128]{2,1,3,0:T(8,128)S(1)} fusion(f32[128,8,64]{2,1,0:T(8,128)S(1)} %fusion.4, f32[8,64,128]{1,0,2:T(8,128)S(1)} %copy.87, f32[64,128]{0,1:T(8,128)S(1)} %copy.85, f32[64,128]{0,1:T(8,128)S(1)} %copy.84, f32[64,128]{0,1:T(8,128)S(1)} %copy.83, f32[64,128]{0,1:T(8,128)S(1)} %copy.82, f32[64,128]{0,1:T(8,128)S(1)} %copy.81, ...), kind=kOutput, calls=%fused_computation.48 | convolution fusion | flops 55640064 | bytes 983040 | tf_op jit(solution)/shard_map/tsm,ksm->ktm/dot_general | solution.py:163
  165.2 1.1 copy.92
  166.9 0.5 fusion.139
  167.4 0.6 fusion.137
  168.0 22.1 %all-gather.3.cloned.1.call-done = f32[8,8,64,128]{3,2,1,0:T(8,128)} async-done(((f32[2,8,64,128]{3,2,1,0:T(8,128)}), f32[8,8,64,128]{3,2,1,0:T(8,128)}) %all-gather.3.cloned.1.call-update) | async-done | bytes 2097168 | tf_op jit(solution)/shard_map/all_gather | solution.py:12
  190.2 1.8 reduce_sum.48
  192.0 0.6 convolution_bitcast_fusion.1
  192.7 0.2 copy.97
  192.9 0.2 copy.96
  193.3 1.0 convolution_bitcast_fusion
  194.4 0.2 copy.100
  194.5 0.2 copy.99
  194.8 0.8 pad_maximum_fusion.1
  (80 shorter events, 4.5 us)
Async XLA Ops:
  6.5 15.2 %copy-start = (f32[2,8,64,128]{3,2,1,0:T(8,128)S(1)}, f32[2,8,64,128]{3,2,1,0:T(8,128)}, u32[]{:S(2)}) copy-start(f32[2,8,64,128]{3,2,1,0:T(8,128)} %param.3) | copy-start | bytes 1572868
  6.5 7.2 %copy-start.1 = (s32[64]{0:T(128)S(1)}, s32[64]{0:T(128)}, u32[]{:S(2)}) copy-start(s32[64]{0:T(128)} %param.5) | copy-start | bytes 772
  6.5 183.6 %all-gather.3.cloned.1.call-start = ((), (), s32[]{:S(2)}) async-start(), calls=%async_computation | async-start | bytes 2621440 | tf_op jit(solution)/shard_map/all_gather | solution.py:12
  6.5 15.2 %collective-permute-start = (f32[1,2,8,64,128]{4,3,2,1,0:T(8,128)}, f32[1,2,8,64,128]{4,3,2,1,0:T(8,128)S(1)}, u32[]{:S(2)}, u32[]{:S(2)}) collective-permute-start(f32[1,2,8,64,128]{4,3,2,1,0:T(8,128)} %bitcast.160), channel_id=1, source_target_pairs={{0,1},{1,0},{2,3},{3,2},{4,5},{5,4},{6,7},{7,6},{8,9},{9,8},{10,11... | collective-permute-start | bytes 1572872 | tf_op jit(solution)/shard_map/ppermute | solution.py:24
  21.9 24.4 %collective-permute-start.1 = (f32[2,2,8,64,128]{4,3,2,1,0:T(8,128)S(1)}, f32[2,2,8,64,128]{4,3,2,1,0:T(8,128)S(1)}, u32[]{:S(2)}, u32[]{:S(2)}) collective-permute-start(f32[2,2,8,64,128]{4,3,2,1,0:T(8,128)S(1)} %maximum_select_fusion.1), channel_id=1, source_target_pairs={{0,2},{2,0},{1,3},{3,1},{4,6},{6,4},{5,7},{7,5},{8,10},{10,8},{9,1... | collective-permute-start | bytes 3145736 | tf_op jit(solution)/shard_map/ppermute | solution.py:24
Sparse Core Ops, SparseCore 0:
  166.5 23.6 all-gather.2
